TPU v7x, 32 devices: a whole 2x2x4 slice. The times are simulated.
32 devices in a mesh: guide: 2 (over core), blk: 16 (over z, y, x).
Axes of the slice: x: 2, y: 2, z: 4, core: 2. Of those that a mesh axis runs over, the one named last changes fastest.
Arguments:
- x_cols: bfloat16 [128, 2048], P(None, 'blk'), may hold values from -3 to 3
- queries: bfloat16 [128, 9216], P('blk'), may hold values from -64 to 64
- new_kv: bfloat16 [128, 576], P('blk'), may hold values from -6 to 6
- cache: bfloat16 [2, 128, 256, 576], P('guide', 'blk'), may hold values from -8 to 8
- lengths: int32 [2, 128], P('guide'), may hold values from 2 to 256, as said below
- perm: int32 [128], replicated, may hold values from 0 to 127, each once
- guide_scale: float32 [128], replicated, may hold values from 1.5 to 7.5
- w_uv: bfloat16 [16, 512, 128], replicated, may hold values from -0.75 to 0.75
- w_out: bfloat16 [2048, 2048], P(None, 'blk'), may hold values from -0.125 to 0.125
- mlp_gain: float32 [2048], replicated, may hold values from 0.5 to 1.5
- w_gate: bfloat16 [2048, 10944], P(None, 'blk'), may hold values from -0.125 to 0.125
- w_up: bfloat16 [2048, 10944], P(None, 'blk'), may hold values from -0.125 to 0.125
- w_down: bfloat16 [10944, 2048], P('blk'), may hold values from -0.0546875 to 0.0546875
- head_gain: float32 [2048], replicated, may hold values from 0.5 to 1.5
- w_head: bfloat16 [2048, 102400], P(None, 'blk'), may hold values from -0.125 to 0.125
Outputs:
- guided: bfloat16 [128, 102400], P('guide', 'blk')
Inputs may be any that keep to these rules, and one draw needn't show every extreme that they name: Positions 0 to lengths[g, r] - 1 of request r's cache in group g are live; each group has a request with 256 live positions. Slot s holds request perm[s]; every request has one slot.
All inputs are finite; a program needn't handle non-finite values.
Results may differ from a plain program's by a relative error of at most 0.018.
Values may be sent and summed in bfloat16 or wider, within the bound.
No kernel may reach another device: no remote copies, remote signals or barrier semaphores. Data moves between devices by JAX's collectives and lax.ppermute only.
A program may use at most 128 MiB of HBM per device.

v0:
```python
import jax
import jax.numpy as jnp
from jax import lax
from jax.sharding import PartitionSpec as P

FF = 10944


def partner(value, axis, apart):
    mask = 2**apart
    pairs = [(source, source ^ mask) for source in range(lax.axis_size(axis))]
    return lax.ppermute(value, axis, pairs)


def rms_round(hidden, gain):
    values = hidden.astype(jnp.float32)
    meansq = jnp.mean(values * values, axis=-1, keepdims=True)
    return (values * lax.rsqrt(meansq + 1e-06) * gain).astype(jnp.bfloat16)


def body(
    x_cols,
    queries,
    new_kv,
    cache,
    lengths,
    perm,
    guide_scale,
    w_uv,
    w_out,
    mlp_gain,
    w_gate,
    w_up,
    w_down,
    head_gain,
    w_head,
):
    guide_index = lax.axis_index("guide")
    blk_index = lax.axis_index("blk")
    slots_dev = queries.shape[0]
    heads_count = w_uv.shape[0]
    latent_size = w_uv.shape[1]
    key_width = new_kv.shape[1]
    score_scale = (w_uv.shape[2] + key_width - latent_size) ** (-0.5)
    slot_ids = blk_index * slots_dev + jnp.arange(slots_dev, dtype=jnp.int32)
    owners = jnp.take(perm, slot_ids)
    live_len = jnp.take(lengths[0], owners)
    query_heads = queries.reshape(slots_dev, heads_count, key_width)
    cached_keys = cache[0]
    scores = (
        jnp.einsum("shk,slk->shl", query_heads, cached_keys, preferred_element_type=jnp.float32)
        * score_scale
    )
    own_score = (
        jnp.einsum("shk,sk->sh", query_heads, new_kv, preferred_element_type=jnp.float32)
        * score_scale
    )
    live_mask = (
        jnp.arange(cached_keys.shape[1], dtype=jnp.int32)[None, None, :] < live_len[:, None, None]
    )
    scores = jnp.where(live_mask, scores, jnp.float32(-1e30))
    peak_score = jnp.maximum(jnp.max(scores, axis=-1), own_score)
    probs = jnp.where(live_mask, jnp.exp(scores - peak_score[..., None]), jnp.float32(0.0))
    own_prob = jnp.exp(own_score - peak_score)
    softmax_total = jnp.sum(probs, axis=-1) + own_prob
    weights = (probs / softmax_total[..., None]).astype(jnp.bfloat16)
    own_weight = (own_prob / softmax_total).astype(jnp.bfloat16)
    latent_out = jnp.einsum(
        "shl,slc->shc", weights, cached_keys[:, :, :latent_size], preferred_element_type=jnp.float32
    )
    latent_out = latent_out + own_weight.astype(jnp.float32)[..., None] * new_kv[
        :, None, :latent_size
    ].astype(jnp.float32)
    value_rows = jnp.einsum(
        "shc,hcd->shd", latent_out.astype(jnp.bfloat16), w_uv, preferred_element_type=jnp.float32
    )
    value_rows = value_rows.astype(jnp.bfloat16).reshape(slots_dev, -1)
    attended = jnp.dot(
        lax.all_gather(value_rows, "blk", axis=0, tiled=True),
        w_out,
        preferred_element_type=jnp.float32,
    )
    residual = (x_cols.astype(jnp.float32) + attended).astype(jnp.bfloat16)
    rows_full = lax.all_gather(residual, "blk", axis=1, tiled=True)
    normed = rms_round(rows_full, mlp_gain)
    unit_count = w_gate.shape[1]
    gate_out = jnp.dot(normed, w_gate, preferred_element_type=jnp.float32)
    up_out = jnp.dot(normed, w_up, preferred_element_type=jnp.float32)
    unit_ids = blk_index * unit_count + jnp.arange(unit_count, dtype=jnp.int32)
    hidden = jnp.where(
        unit_ids[None, :] < FF, jax.nn.silu(gate_out) * up_out, jnp.float32(0.0)
    ).astype(jnp.bfloat16)
    partial_sum = jnp.dot(hidden, w_down, preferred_element_type=jnp.float32)
    summed = lax.psum(partial_sum, "blk")
    after_mlp = (rows_full.astype(jnp.float32) + summed).astype(jnp.bfloat16)
    logits = jnp.dot(rms_round(after_mlp, head_gain), w_head, preferred_element_type=jnp.float32)
    request_count = logits.shape[0]
    half_rows = request_count // 2
    slot_scale = jnp.take(guide_scale, perm)
    request_order = (
        jnp.zeros((request_count,), jnp.int32)
        .at[perm]
        .set(jnp.arange(request_count, dtype=jnp.int32))
    )
    own_order = lax.dynamic_slice_in_dim(request_order, guide_index * half_rows, half_rows)
    other_logits = partner(logits.astype(jnp.bfloat16), "guide", 0).astype(logits.dtype)
    cond_logits = jnp.where(guide_index == 0, logits, other_logits)
    uncond_logits = jnp.where(guide_index == 0, other_logits, logits)
    mixed = (uncond_logits + slot_scale[:, None] * (cond_logits - uncond_logits)).astype(
        jnp.bfloat16
    )
    return jnp.take(mixed, own_order, axis=0)


def solution(mesh):
    return jax.shard_map(
        body,
        mesh=mesh,
        in_specs=(
            P(None, "blk"),
            P("blk", None),
            P("blk", None),
            P("guide", "blk", None, None),
            P("guide", None),
            P(),
            P(),
            P(),
            P(None, "blk"),
            P(),
            P(None, "blk"),
            P(None, "blk"),
            P("blk", None),
            P(),
            P(None, "blk"),
        ),
        out_specs=P("guide", "blk"),
        check_vma=False,
    )
```

profile of v0, /device:TPU:0, one launch (start us, length us, event | category | flops | bytes accessed | tf_op | source)
XLA Modules:
  0.0 257.7 jit_solution(10083849745343940406)
XLA Ops:
  6.5 0.0 copy-start
  6.5 0.0 all-reduce.2.cloned.1.call-start
  6.5 1.2 reshape.73
  7.8 1.3 gather_fusion.2
  9.1 1.3 gather_fusion.3
  10.4 0.1 iota_compare_fusion
  10.5 0.7 slice_convert_fusion
  11.2 0.9 fusion.44
  12.1 2.2 fusion.55
  14.3 0.2 fusion.39
  14.5 0.1 copy.17
  14.6 0.0 copy-start.3
  14.6 0.0 copy-start.4
  14.6 0.0 copy-start.6
  14.6 2.4 fusion.4
  17.0 0.0 copy-done.3
  17.0 0.0 copy-start.7
  17.0 0.5 fusion.11
  17.5 45.3 %all_gather.6 = bf16[128,2048]{1,0:T(8,128)(2,1)S(1)} all-gather(bf16[8,2048]{1,0:T(8,128)(2,1)S(1)} %fusion.11), channel_id=1, replica_groups=mesh['guide'=2,'blk'=16] {'blk'}, dimensions={0}, use_global_device_ids=true | all-gather | bytes 557056 | tf_op jit(solution)/shard_map/all_gather | solution.py:79
  62.8 0.0 copy-done.4
  62.8 0.0 copy-done.6
  62.8 0.3 fusion.10
  63.1 38.5 %all_gather.7 = bf16[128,2048]{1,0:T(8,128)(2,1)S(1)} all-gather(bf16[128,128]{1,0:T(8,128)(2,1)S(1)} %fusion.10), channel_id=1, replica_groups=mesh['guide'=2,'blk'=16] {'blk'}, dimensions={1}, use_global_device_ids=true | all-gather | bytes 557056 | tf_op jit(solution)/shard_map/all_gather | solution.py:84
  101.7 0.2 fusion.15
  101.9 0.0 copy-done.7
  101.9 3.5 %fusion.34 = f32[128,684]{0,1:T(8,128)} fusion(bf16[2048,684]{0,1:T(8,128)(2,1)} %param.27, bf16[128,2048]{1,0:T(8,128)(2,1)S(1)} %all_gather.7, f32[2048]{0:T(1024)S(1)} %copy-done.7, f32[128]{0:T(128)S(1)} %add_rsqrt_fusion.1), kind=kOutput, calls=%fused_computation.49 | convolution fusion | flops 359661568 | bytes 3684864 | tf_op jit(solution)/shard_map/dot_general | solution.py:87
  105.4 0.0 copy-done
  105.4 0.0 copy-start.5
  105.4 5.0 %fusion.8 = f32[128,2048]{1,0:T(8,128)} fusion(bf16[684,2048]{1,0:T(8,128)(2,1)S(1)} %copy-done, bf16[2048,684]{0,1:T(8,128)(2,1)} %param.28, f32[128,684]{0,1:T(8,128)} %fusion.34, pred[684]{0:T(1024)(128)(4,1)S(1)} %add_compare_fusion, bf16[128,2048]{1,0:T(8,128)(2,1)S(1)} %all_gather.7, f32[2048]{0:T(1024)S(1)} %copy-done.7, f32[128]{0:T(128)S(1)} %add_rsqrt_fusion.1), kind=kOutput, calls=%fused_computation.21 | convolution fusion | flops 718887424 | bytes 7535788 | tf_op jit(solution)/shard_map/dot_general | solution.py:93
  110.4 0.0 all-reduce.2.cloned.1.call-update
  110.5 109.6 %all-reduce.2.cloned.1.call-done = f32[128,2048]{1,0:T(8,128)} async-done(((f32[128,2048]{1,0:T(8,128)}), f32[128,2048]{1,0:T(8,128)}) %all-reduce.2.cloned.1.call-update) | async-done | bytes 1048592 | tf_op jit(solution)/shard_map/psum | solution.py:94
  220.1 1.4 fusion.12
  221.5 0.0 copy-done.5
  221.5 0.0 copy-start.2
  221.5 0.0 copy-start.1
  221.5 14.7 %fusion.56 = (bf16[128,6400]{1,0:T(8,128)(2,1)}, f32[128,6400]{1,0:T(8,128)}) fusion(bf16[2048,6400]{1,0:T(8,128)(2,1)} %param.31, f32[2048]{0:T(1024)S(1)} %copy-done.5, f32[128]{0:T(128)S(1)} %add_rsqrt_fusion, f32[128,2048]{1,0:T(8,128)} %all-reduce.2.cloned.1.call-done, bf16[128,2048]{1,0:T(8,128)(2,1)S(1)} %all_gather.7), kind=kOutput, calls=%fused_computation.90 | convolution fusion | flops 3358097408 | bytes 32711168 | tf_op jit(solution)/shard_map/dot_general | solution.py:96
  236.2 0.0 collective-permute-start
  236.2 0.0 copy-done.2
  236.2 1.2 scatter_custom_fusion
  237.4 0.0 copy-done.1
  237.4 1.2 gather_fusion
  238.6 0.1 compare_and_fusion
  238.8 1.3 collective-permute-done
  240.1 4.3 %fusion.3 = bf16[128,6400]{1,0:T(8,128)(2,1)} fusion(f32[128,6400]{1,0:T(8,128)} %get-tuple-element.13, bf16[128,6400]{1,0:T(8,128)(2,1)} %collective-permute-done, f32[128]{0:T(128)S(1)} %and_select_fusion.2, pred[]{:T(512)S(6)} %eq.4), kind=kLoop, calls=%fused_computation.10 | loop fusion | flops 5734400 | bytes 6554113 | tf_op jit(solution)/shard_map/convert_element_type | solution.py:109
  244.4 4.3 %gather_fusion.1 = bf16[64,6400]{1,0:T(8,128)(2,1)} fusion(bf16[128,6400]{1,0:T(8,128)(2,1)} %fusion.3, s32[1024]{0:T(1024)S(1)} %pad_clamp_fusion), kind=kCustom, calls=%fused_computation.3 | custom fusion | bytes 1638656 | tf_op jit(solution)/shard_map/jit(_take)/gather | solution.py:112
  248.7 2.2 broadcast_select_fusion
  (15 shorter events, 0.1 us)
Async XLA Ops:
  6.5 98.9 %copy-start = (bf16[684,2048]{1,0:T(8,128)(2,1)S(1)}, bf16[684,2048]{1,0:T(8,128)(2,1)}, u32[]{:S(2)}) copy-start(bf16[684,2048]{1,0:T(8,128)(2,1)} %param.29) | copy-start | bytes 8404996
  6.5 213.5 %all-reduce.2.cloned.1.call-start = ((), (), s32[]{:S(2)}) async-start(), calls=%async_computation | async-start | bytes 2097152 | tf_op jit(solution)/shard_map/psum | solution.py:94
  14.6 2.4 copy-start.3
  14.6 48.3 %copy-start.4 = (bf16[2048,128]{1,0:T(8,128)(2,1)S(1)}, bf16[2048,128]{1,0:T(8,128)(2,1)}, u32[]{:S(2)}) copy-start(bf16[2048,128]{1,0:T(8,128)(2,1)} %param.25) | copy-start | bytes 1572868
  14.6 48.3 %copy-start.6 = (bf16[128,128]{1,0:T(8,128)(2,1)S(1)}, bf16[128,128]{1,0:T(8,128)(2,1)}, u32[]{:S(2)}) copy-start(bf16[128,128]{1,0:T(8,128)(2,1)} %param.17) | copy-start | bytes 98308
  17.0 84.9 %copy-start.7 = (f32[2048]{0:T(1024)S(1)}, f32[2048]{0:T(1024)}, u32[]{:S(2)}) copy-start(f32[2048]{0:T(1024)} %param.26) | copy-start | bytes 24580
  105.4 116.1 %copy-start.5 = (f32[2048]{0:T(1024)S(1)}, f32[2048]{0:T(1024)}, u32[]{:S(2)}) copy-start(f32[2048]{0:T(1024)} %param.30) | copy-start | bytes 24580
  221.5 14.7 %copy-start.2 = (s32[128]{0:T(128)S(1)}, s32[128]{0:T(128)}, u32[]{:S(2)}) copy-start(s32[128]{0:T(128)} %param.22) | copy-start | bytes 1540
  221.5 15.9 %copy-start.1 = (f32[128]{0:T(128)S(1)}, f32[128]{0:T(128)}, u32[]{:S(2)}) copy-start(f32[128]{0:T(128)} %param.23) | copy-start | bytes 1540
  236.2 3.8 %collective-permute-start = (bf16[128,6400]{1,0:T(8,128)(2,1)}, bf16[128,6400]{1,0:T(8,128)(2,1)}, u32[]{:S(2)}, u32[]{:S(2)}) collective-permute-start(bf16[128,6400]{1,0:T(8,128)(2,1)} %get-tuple-element.12), channel_id=1, source_target_pairs={{0,16},{16,0},{1,17},{17,1},{2,18},{18,2},{3,19},{19,3},{4,20},{20... | collective-permute-start | bytes 4915208 | tf_op jit(solution)/shard_map/ppermute | solution.py:12
Sparse Core Ops, SparseCore 0:
  110.6 109.4 all-reduce.1
where the time goes:
time: 258 us
  waiting for transfers between devices  111 us (43%)
  blocking collectives  83.9 us (33%)
  matrix products  29.5 us (11%)
  between operations  13.5 us (5%)
  local copies, waits for them, and re-layouts  10.7 us (4%)
  other arithmetic  9.26 us (4%)
    psum x1, waiting for transfers between devices, body(): summed = lax.psum(partial_sum, 'blk')  110 us
    all_gather x1, blocking collectives, body(): lax.all_gather(value_rows, 'blk', axis=0, tiled=True)  45.3 us
    all_gather x1, blocking collectives, body(): rows_full = lax.all_gather(residual, 'blk', axis=1, tiled=True)  38.5 us
    dot_general x1, matrix products, body(): jnp.dot(rms_round(after_mlp, head_gain), w_head, preferred_element_type=j...  14.7 us
  transfers between devices with their start and end apart: 2, of which 2 were waited for; matrix products, arithmetic and copies ran while one was open for 1% of the time, Pallas kernels for 0%

commit v1 on v0

--- a/solution.py
+++ b/solution.py
@@ -81,7 +81,12 @@
         preferred_element_type=jnp.float32,
     )
     residual = (x_cols.astype(jnp.float32) + attended).astype(jnp.bfloat16)
-    rows_full = lax.all_gather(residual, "blk", axis=1, tiled=True)
+    ring = [residual]
+    for hop in range(15):
+        ring.append(lax.ppermute(ring[-1], "blk", [(dev, (dev + 1) % 16) for dev in range(16)]))
+    rows_full = jnp.roll(
+        jnp.concatenate(ring[::-1], axis=1), (lax.axis_index("blk") + 1) * ring[0].shape[1], axis=1
+    )
     normed = rms_round(rows_full, mlp_gain)
     unit_count = w_gate.shape[1]
     gate_out = jnp.dot(normed, w_gate, preferred_element_type=jnp.float32)

time: 258 us -> 335 us (1.30)
  waiting for transfers between devices: 111 us -> 222 us
  blocking collectives: 83.9 us -> 45.3 us
    ppermute x0 -> x15, waiting for transfers between devices: none -> 113 us  [body(): lax.ppermute(ring[-1], 'blk', [(dev, (dev + 1) % 16) for dev in range(16)])]
    all_gather x1 -> x0, blocking collectives: 38.5 us -> none  [body(): rows_full = lax.all_gather(residual, 'blk', axis=1, tiled=True)]
  transfers between devices with their start and end apart: 2 -> 17, of which waited for: 2 -> 17; matrix products, arithmetic and copies ran while one was open for 1% -> 1% of each run, Pallas kernels for 0% -> 0%
where the time goes in v1:
time: 335 us; the launch traced here: 334 us
  waiting for transfers between devices  222 us (66%)
  blocking collectives  45.3 us (14%)
  matrix products  30.9 us (9%)
  between operations  13.7 us (4%)
  local copies, waits for them, and re-layouts  11.6 us (3%)
  other arithmetic  10.3 us (3%)
    ppermute x15, waiting for transfers between devices, body(): lax.ppermute(ring[-1], 'blk', [(dev, (dev + 1) % 16) for dev in range(16)])  113 us
    psum x1, waiting for transfers between devices, body(): summed = lax.psum(partial_sum, 'blk')  108 us
    all_gather x1, blocking collectives, body(): lax.all_gather(value_rows, 'blk', axis=0, tiled=True)  45.3 us
    dot_general x1, matrix products, body(): jnp.dot(rms_round(after_mlp, head_gain), w_head, preferred_element_type=j...  14.6 us
  transfers between devices with their start and end apart: 17, of which 17 were waited for; matrix products, arithmetic and copies ran while one was open for 1% of the time, Pallas kernels for 0%

profile of v1, /device:TPU:0, one launch (start us, length us, event | category | flops | bytes accessed | tf_op | source)
XLA Modules:
  0.0 334.2 jit_solution(17433428767667814144)
XLA Ops:
  6.5 1.2 reshape.73
  7.8 0.7 compare_select_fusion.3
  8.5 1.3 gather_fusion.2
  9.8 1.3 gather_fusion.3
  11.1 0.1 iota_compare_fusion
  11.2 0.7 slice_convert_fusion
  11.9 0.9 fusion.44
  12.7 2.2 fusion.58
  14.9 0.2 fusion.35
  15.1 0.1 copy.20
  15.2 2.4 fusion.4
  17.6 0.5 fusion.11
  18.1 45.3 %all_gather.3 = bf16[128,2048]{1,0:T(8,128)(2,1)S(1)} all-gather(bf16[8,2048]{1,0:T(8,128)(2,1)S(1)} %fusion.11), channel_id=1, replica_groups=mesh['guide'=2,'blk'=16] {'blk'}, dimensions={0}, use_global_device_ids=true | all-gather | bytes 557056 | tf_op jit(solution)/shard_map/all_gather | solution.py:79
  63.5 0.1 copy.19
  63.6 1.4 fusion.10
  65.0 0.1 collective-permute-start
  65.1 7.5 %collective-permute-done = bf16[128,128]{0,1:T(8,128)(2,1)S(1)} collective-permute-done((bf16[128,128]{0,1:T(8,128)(2,1)S(1)}, bf16[128,128]{0,1:T(8,128)(2,1)S(1)}, u32[]{:S(2)}, u32[]{:S(2)}) %collective-permute-start) | collective-permute-done | bytes 32800 | tf_op jit(solution)/shard_map/ppermute | solution.py:86
  72.6 7.5 %collective-permute-done.1 = bf16[128,128]{0,1:T(8,128)(2,1)S(1)} collective-permute-done((bf16[128,128]{0,1:T(8,128)(2,1)S(1)}, bf16[128,128]{0,1:T(8,128)(2,1)S(1)}, u32[]{:S(2)}, u32[]{:S(2)}) %collective-permute-start.1) | collective-permute-done | bytes 32800 | tf_op jit(solution)/shard_map/ppermute | solution.py:86
  80.1 7.5 %collective-permute-done.2 = bf16[128,128]{0,1:T(8,128)(2,1)S(1)} collective-permute-done((bf16[128,128]{0,1:T(8,128)(2,1)S(1)}, bf16[128,128]{0,1:T(8,128)(2,1)S(1)}, u32[]{:S(2)}, u32[]{:S(2)}) %collective-permute-start.2) | collective-permute-done | bytes 32800 | tf_op jit(solution)/shard_map/ppermute | solution.py:86
  87.6 7.5 %collective-permute-done.3 = bf16[128,128]{0,1:T(8,128)(2,1)S(1)} collective-permute-done((bf16[128,128]{0,1:T(8,128)(2,1)S(1)}, bf16[128,128]{0,1:T(8,128)(2,1)S(1)}, u32[]{:S(2)}, u32[]{:S(2)}) %collective-permute-start.3) | collective-permute-done | bytes 32800 | tf_op jit(solution)/shard_map/ppermute | solution.py:86
  95.1 7.8 %collective-permute-done.4 = bf16[128,128]{0,1:T(8,128)(2,1)S(1)} collective-permute-done((bf16[128,128]{0,1:T(8,128)(2,1)S(1)}, bf16[128,128]{0,1:T(8,128)(2,1)S(1)}, u32[]{:S(2)}, u32[]{:S(2)}) %collective-permute-start.4) | collective-permute-done | bytes 32800 | tf_op jit(solution)/shard_map/ppermute | solution.py:86
  102.9 7.5 %collective-permute-done.5 = bf16[128,128]{0,1:T(8,128)(2,1)S(1)} collective-permute-done((bf16[128,128]{0,1:T(8,128)(2,1)S(1)}, bf16[128,128]{0,1:T(8,128)(2,1)S(1)}, u32[]{:S(2)}, u32[]{:S(2)}) %collective-permute-start.5) | collective-permute-done | bytes 32800 | tf_op jit(solution)/shard_map/ppermute | solution.py:86
  110.4 7.5 %collective-permute-done.6 = bf16[128,128]{0,1:T(8,128)(2,1)S(1)} collective-permute-done((bf16[128,128]{0,1:T(8,128)(2,1)S(1)}, bf16[128,128]{0,1:T(8,128)(2,1)S(1)}, u32[]{:S(2)}, u32[]{:S(2)}) %collective-permute-start.6) | collective-permute-done | bytes 32800 | tf_op jit(solution)/shard_map/ppermute | solution.py:86
  117.9 7.5 %collective-permute-done.7 = bf16[128,128]{0,1:T(8,128)(2,1)S(1)} collective-permute-done((bf16[128,128]{0,1:T(8,128)(2,1)S(1)}, bf16[128,128]{0,1:T(8,128)(2,1)S(1)}, u32[]{:S(2)}, u32[]{:S(2)}) %collective-permute-start.7) | collective-permute-done | bytes 32800 | tf_op jit(solution)/shard_map/ppermute | solution.py:86
  125.4 7.5 %collective-permute-done.8 = bf16[128,128]{0,1:T(8,128)(2,1)S(1)} collective-permute-done((bf16[128,128]{0,1:T(8,128)(2,1)S(1)}, bf16[128,128]{0,1:T(8,128)(2,1)S(1)}, u32[]{:S(2)}, u32[]{:S(2)}) %collective-permute-start.8) | collective-permute-done | bytes 32800 | tf_op jit(solution)/shard_map/ppermute | solution.py:86
  132.9 7.5 %collective-permute-done.9 = bf16[128,128]{0,1:T(8,128)(2,1)S(1)} collective-permute-done((bf16[128,128]{0,1:T(8,128)(2,1)S(1)}, bf16[128,128]{0,1:T(8,128)(2,1)S(1)}, u32[]{:S(2)}, u32[]{:S(2)}) %collective-permute-start.9) | collective-permute-done | bytes 32800 | tf_op jit(solution)/shard_map/ppermute | solution.py:86
  140.4 7.6 %collective-permute-done.10 = bf16[128,128]{0,1:T(8,128)(2,1)S(1)} collective-permute-done((bf16[128,128]{0,1:T(8,128)(2,1)S(1)}, bf16[128,128]{0,1:T(8,128)(2,1)S(1)}, u32[]{:S(2)}, u32[]{:S(2)}) %collective-permute-start.10) | collective-permute-done | bytes 32800 | tf_op jit(solution)/shard_map/ppermute | solution.py:86
  148.1 7.5 %collective-permute-done.11 = bf16[128,128]{0,1:T(8,128)(2,1)S(1)} collective-permute-done((bf16[128,128]{0,1:T(8,128)(2,1)S(1)}, bf16[128,128]{0,1:T(8,128)(2,1)S(1)}, u32[]{:S(2)}, u32[]{:S(2)}) %collective-permute-start.11) | collective-permute-done | bytes 32800 | tf_op jit(solution)/shard_map/ppermute | solution.py:86
  155.6 7.5 %collective-permute-done.12 = bf16[128,128]{0,1:T(8,128)(2,1)S(1)} collective-permute-done((bf16[128,128]{0,1:T(8,128)(2,1)S(1)}, bf16[128,128]{0,1:T(8,128)(2,1)S(1)}, u32[]{:S(2)}, u32[]{:S(2)}) %collective-permute-start.12) | collective-permute-done | bytes 32800 | tf_op jit(solution)/shard_map/ppermute | solution.py:86
  163.1 7.5 %collective-permute-done.13 = bf16[128,128]{0,1:T(8,128)(2,1)S(1)} collective-permute-done((bf16[128,128]{0,1:T(8,128)(2,1)S(1)}, bf16[128,128]{0,1:T(8,128)(2,1)S(1)}, u32[]{:S(2)}, u32[]{:S(2)}) %collective-permute-start.13) | collective-permute-done | bytes 32800 | tf_op jit(solution)/shard_map/ppermute | solution.py:86
  170.6 7.5 %collective-permute-done.14 = bf16[128,128]{0,1:T(8,128)(2,1)S(1)} collective-permute-done((bf16[128,128]{0,1:T(8,128)(2,1)S(1)}, bf16[128,128]{0,1:T(8,128)(2,1)S(1)}, u32[]{:S(2)}, u32[]{:S(2)}) %collective-permute-start.14) | collective-permute-done | bytes 32800 | tf_op jit(solution)/shard_map/ppermute | solution.py:86
  178.6 0.3 fusion.15
  178.9 0.7 copy-done.3
  179.6 2.8 fusion.38
  182.4 6.2 %fusion.8 = f32[128,2048]{0,1:T(8,128)} fusion(bf16[684,2048]{1,0:T(8,128)(2,1)S(1)} %copy-done, bf16[2048,684]{0,1:T(8,128)(2,1)} %param.28, f32[128,684]{0,1:T(8,128)S(1)} %fusion.38, pred[684]{0:T(1024)(128)(4,1)S(1)} %add_compare_fusion, f32[2048]{0:T(1024)S(1)} %copy-done.7, f32[128]{0:T(128)S(1)} %add_rsqrt_fusion.1, bf16[128,4096]{0,1:T(8,128)(2,1)} %copy-done.3, ...), kind=kOutput, calls=%fused_computation.21 | convolution fusion | flops 718887424 | bytes 7552176 | tf_op jit(solution)/shard_map/dot_general | solution.py:98
  188.5 0.0 all-reduce.2.cloned.1.call-update
  188.6 107.7 %all-reduce.2.cloned.1.call-done = f32[128,2048]{0,1:T(8,128)} async-done(((f32[128,2048]{0,1:T(8,128)}), f32[128,2048]{0,1:T(8,128)}) %all-reduce.2.cloned.1.call-update) | async-done | bytes 1048592 | tf_op jit(solution)/shard_map/psum | solution.py:99
  296.3 1.6 fusion.12
  297.9 0.0 copy-start.1
  298.0 0.0 copy-start.2
  298.0 14.6 %fusion.59 = (bf16[128,6400]{1,0:T(8,128)(2,1)}, f32[128,6400]{1,0:T(8,128)}) fusion(bf16[2048,6400]{1,0:T(8,128)(2,1)} %param.31, bf16[128,2048]{0,1:T(8,128)(2,1)S(1)} %get-tuple-element.9, f32[2048]{0:T(1024)S(1)} %copy-done.5, f32[128]{0:T(128)S(1)} %add_rsqrt_fusion), kind=kOutput, calls=%fused_computation.124 | convolution fusion | flops 3357310976 | bytes 31662592 | tf_op jit(solution)/shard_map/dot_general | solution.py:101
  312.6 1.0 scatter_custom_fusion
  313.6 1.2 gather_fusion
  314.8 0.1 compare_and_fusion
  314.9 1.5 collective-permute-done.15
  316.4 4.4 %fusion.3 = bf16[128,6400]{1,0:T(8,128)(2,1)} fusion(f32[128,6400]{1,0:T(8,128)} %get-tuple-element.15, bf16[128,6400]{1,0:T(8,128)(2,1)} %collective-permute-done.15, f32[128]{0:T(128)S(1)} %and_select_fusion.2, pred[]{:T(512)S(6)} %eq.7), kind=kLoop, calls=%fused_computation.10 | loop fusion | flops 5734400 | bytes 6554113 | tf_op jit(solution)/shard_map/convert_element_type | solution.py:114
  320.8 4.3 %gather_fusion.1 = bf16[64,6400]{1,0:T(8,128)(2,1)} fusion(bf16[128,6400]{1,0:T(8,128)(2,1)} %fusion.3, s32[1024]{0:T(1024)S(1)} %pad_clamp_fusion), kind=kCustom, calls=%fused_computation.3 | custom fusion | bytes 1638656 | tf_op jit(solution)/shard_map/jit(_take)/gather | solution.py:117
  325.1 2.2 broadcast_select_fusion
  (74 shorter events, 0.5 us)
Async XLA Ops:
  6.5 175.8 %copy-start = (bf16[684,2048]{1,0:T(8,128)(2,1)S(1)}, bf16[684,2048]{1,0:T(8,128)(2,1)}, u32[]{:S(2)}) copy-start(bf16[684,2048]{1,0:T(8,128)(2,1)} %param.29) | copy-start | bytes 8404996
  6.5 289.7 %all-reduce.2.cloned.1.call-start = ((), (), s32[]{:S(2)}) async-start(), calls=%async_computation | async-start | bytes 2097152 | tf_op jit(solution)/shard_map/psum | solution.py:99
  15.2 2.4 copy-start.4
  15.2 48.3 %copy-start.6 = (bf16[128,128]{1,0:T(8,128)(2,1)S(1)}, bf16[128,128]{1,0:T(8,128)(2,1)}, u32[]{:S(2)}) copy-start(bf16[128,128]{1,0:T(8,128)(2,1)} %param.17) | copy-start | bytes 98308
  17.6 161.9 %copy-start.7 = (f32[2048]{0:T(1024)S(1)}, f32[2048]{0:T(1024)}, u32[]{:S(2)}) copy-start(f32[2048]{0:T(1024)} %param.26) | copy-start | bytes 24580
  65.0 7.6 %collective-permute-start = (bf16[128,128]{0,1:T(8,128)(2,1)S(1)}, bf16[128,128]{0,1:T(8,128)(2,1)S(1)}, u32[]{:S(2)}, u32[]{:S(2)}) collective-permute-start(bf16[128,128]{0,1:T(8,128)(2,1)S(1)} %fusion.10), channel_id=1, source_target_pairs={{0,1},{1,2},{2,3},{3,4},{4,5},{5,6},{6,7},{7,8},{8,9},{9,10},{10,1... | collective-permute-start | bytes 98312 | tf_op jit(solution)/shard_map/ppermute | solution.py:86
  72.6 7.5 %collective-permute-start.1 = (bf16[128,128]{0,1:T(8,128)(2,1)S(1)}, bf16[128,128]{0,1:T(8,128)(2,1)S(1)}, u32[]{:S(2)}, u32[]{:S(2)}) collective-permute-start(bf16[128,128]{0,1:T(8,128)(2,1)S(1)} %collective-permute-done), channel_id=1, source_target_pairs={{0,1},{1,2},{2,3},{3,4},{4,5},{5,6},{6,7},{7,8},{8,9},{9,10},{10,1... | collective-permute-start | bytes 98312 | tf_op jit(solution)/shard_map/ppermute | solution.py:86
  80.1 7.5 %collective-permute-start.2 = (bf16[128,128]{0,1:T(8,128)(2,1)S(1)}, bf16[128,128]{0,1:T(8,128)(2,1)S(1)}, u32[]{:S(2)}, u32[]{:S(2)}) collective-permute-start(bf16[128,128]{0,1:T(8,128)(2,1)S(1)} %collective-permute-done.1), channel_id=1, source_target_pairs={{0,1},{1,2},{2,3},{3,4},{4,5},{5,6},{6,7},{7,8},{8,9},{9,10},{10,1... | collective-permute-start | bytes 98312 | tf_op jit(solution)/shard_map/ppermute | solution.py:86
  87.6 7.5 %collective-permute-start.3 = (bf16[128,128]{0,1:T(8,128)(2,1)S(1)}, bf16[128,128]{0,1:T(8,128)(2,1)S(1)}, u32[]{:S(2)}, u32[]{:S(2)}) collective-permute-start(bf16[128,128]{0,1:T(8,128)(2,1)S(1)} %collective-permute-done.2), channel_id=1, source_target_pairs={{0,1},{1,2},{2,3},{3,4},{4,5},{5,6},{6,7},{7,8},{8,9},{9,10},{10,1... | collective-permute-start | bytes 98312 | tf_op jit(solution)/shard_map/ppermute | solution.py:86
  95.1 7.8 %collective-permute-start.4 = (bf16[128,128]{0,1:T(8,128)(2,1)S(1)}, bf16[128,128]{0,1:T(8,128)(2,1)S(1)}, u32[]{:S(2)}, u32[]{:S(2)}) collective-permute-start(bf16[128,128]{0,1:T(8,128)(2,1)S(1)} %collective-permute-done.3), channel_id=1, source_target_pairs={{0,1},{1,2},{2,3},{3,4},{4,5},{5,6},{6,7},{7,8},{8,9},{9,10},{10,1... | collective-permute-start | bytes 98312 | tf_op jit(solution)/shard_map/ppermute | solution.py:86
  102.9 7.5 %collective-permute-start.5 = (bf16[128,128]{0,1:T(8,128)(2,1)S(1)}, bf16[128,128]{0,1:T(8,128)(2,1)S(1)}, u32[]{:S(2)}, u32[]{:S(2)}) collective-permute-start(bf16[128,128]{0,1:T(8,128)(2,1)S(1)} %collective-permute-done.4), channel_id=1, source_target_pairs={{0,1},{1,2},{2,3},{3,4},{4,5},{5,6},{6,7},{7,8},{8,9},{9,10},{10,1... | collective-permute-start | bytes 98312 | tf_op jit(solution)/shard_map/ppermute | solution.py:86
  110.4 7.5 %collective-permute-start.6 = (bf16[128,128]{0,1:T(8,128)(2,1)S(1)}, bf16[128,128]{0,1:T(8,128)(2,1)S(1)}, u32[]{:S(2)}, u32[]{:S(2)}) collective-permute-start(bf16[128,128]{0,1:T(8,128)(2,1)S(1)} %collective-permute-done.5), channel_id=1, source_target_pairs={{0,1},{1,2},{2,3},{3,4},{4,5},{5,6},{6,7},{7,8},{8,9},{9,10},{10,1... | collective-permute-start | bytes 98312 | tf_op jit(solution)/shard_map/ppermute | solution.py:86
  117.9 7.5 %collective-permute-start.7 = (bf16[128,128]{0,1:T(8,128)(2,1)S(1)}, bf16[128,128]{0,1:T(8,128)(2,1)S(1)}, u32[]{:S(2)}, u32[]{:S(2)}) collective-permute-start(bf16[128,128]{0,1:T(8,128)(2,1)S(1)} %collective-permute-done.6), channel_id=1, source_target_pairs={{0,1},{1,2},{2,3},{3,4},{4,5},{5,6},{6,7},{7,8},{8,9},{9,10},{10,1... | collective-permute-start | bytes 98312 | tf_op jit(solution)/shard_map/ppermute | solution.py:86
  125.4 7.5 %collective-permute-start.8 = (bf16[128,128]{0,1:T(8,128)(2,1)S(1)}, bf16[128,128]{0,1:T(8,128)(2,1)S(1)}, u32[]{:S(2)}, u32[]{:S(2)}) collective-permute-start(bf16[128,128]{0,1:T(8,128)(2,1)S(1)} %collective-permute-done.7), channel_id=1, source_target_pairs={{0,1},{1,2},{2,3},{3,4},{4,5},{5,6},{6,7},{7,8},{8,9},{9,10},{10,1... | collective-permute-start | bytes 98312 | tf_op jit(solution)/shard_map/ppermute | solution.py:86
  132.9 7.5 %collective-permute-start.9 = (bf16[128,128]{0,1:T(8,128)(2,1)S(1)}, bf16[128,128]{0,1:T(8,128)(2,1)S(1)}, u32[]{:S(2)}, u32[]{:S(2)}) collective-permute-start(bf16[128,128]{0,1:T(8,128)(2,1)S(1)} %collective-permute-done.8), channel_id=1, source_target_pairs={{0,1},{1,2},{2,3},{3,4},{4,5},{5,6},{6,7},{7,8},{8,9},{9,10},{10,1... | collective-permute-start | bytes 98312 | tf_op jit(solution)/shard_map/ppermute | solution.py:86
  140.4 7.6 %collective-permute-start.10 = (bf16[128,128]{0,1:T(8,128)(2,1)S(1)}, bf16[128,128]{0,1:T(8,128)(2,1)S(1)}, u32[]{:S(2)}, u32[]{:S(2)}) collective-permute-start(bf16[128,128]{0,1:T(8,128)(2,1)S(1)} %collective-permute-done.9), channel_id=1, source_target_pairs={{0,1},{1,2},{2,3},{3,4},{4,5},{5,6},{6,7},{7,8},{8,9},{9,10},{10,1... | collective-permute-start | bytes 98312 | tf_op jit(solution)/shard_map/ppermute | solution.py:86
  148.1 7.5 %collective-permute-start.11 = (bf16[128,128]{0,1:T(8,128)(2,1)S(1)}, bf16[128,128]{0,1:T(8,128)(2,1)S(1)}, u32[]{:S(2)}, u32[]{:S(2)}) collective-permute-start(bf16[128,128]{0,1:T(8,128)(2,1)S(1)} %collective-permute-done.10), channel_id=1, source_target_pairs={{0,1},{1,2},{2,3},{3,4},{4,5},{5,6},{6,7},{7,8},{8,9},{9,10},{10,1... | collective-permute-start | bytes 98312 | tf_op jit(solution)/shard_map/ppermute | solution.py:86
  155.6 7.5 %collective-permute-start.12 = (bf16[128,128]{0,1:T(8,128)(2,1)S(1)}, bf16[128,128]{0,1:T(8,128)(2,1)S(1)}, u32[]{:S(2)}, u32[]{:S(2)}) collective-permute-start(bf16[128,128]{0,1:T(8,128)(2,1)S(1)} %collective-permute-done.11), channel_id=1, source_target_pairs={{0,1},{1,2},{2,3},{3,4},{4,5},{5,6},{6,7},{7,8},{8,9},{9,10},{10,1... | collective-permute-start | bytes 98312 | tf_op jit(solution)/shard_map/ppermute | solution.py:86
  163.1 7.5 %collective-permute-start.13 = (bf16[128,128]{0,1:T(8,128)(2,1)S(1)}, bf16[128,128]{0,1:T(8,128)(2,1)S(1)}, u32[]{:S(2)}, u32[]{:S(2)}) collective-permute-start(bf16[128,128]{0,1:T(8,128)(2,1)S(1)} %collective-permute-done.12), channel_id=1, source_target_pairs={{0,1},{1,2},{2,3},{3,4},{4,5},{5,6},{6,7},{7,8},{8,9},{9,10},{10,1... | collective-permute-start | bytes 98312 | tf_op jit(solution)/shard_map/ppermute | solution.py:86
  170.6 7.5 %collective-permute-start.14 = (bf16[128,128]{0,1:T(8,128)(2,1)S(1)}, bf16[128,128]{0,1:T(8,128)(2,1)S(1)}, u32[]{:S(2)}, u32[]{:S(2)}) collective-permute-start(bf16[128,128]{0,1:T(8,128)(2,1)S(1)} %collective-permute-done.13), channel_id=1, source_target_pairs={{0,1},{1,2},{2,3},{3,4},{4,5},{5,6},{6,7},{7,8},{8,9},{9,10},{10,1... | collective-permute-start | bytes 98312 | tf_op jit(solution)/shard_map/ppermute | solution.py:86
  178.6 1.0 copy-start.3
  188.5 109.4 %copy-start.5 = (f32[2048]{0:T(1024)S(1)}, f32[2048]{0:T(1024)}, u32[]{:S(2)}) copy-start(f32[2048]{0:T(1024)} %param.30) | copy-start | bytes 24580
  297.9 15.6 %copy-start.1 = (f32[128]{0:T(128)S(1)}, f32[128]{0:T(128)}, u32[]{:S(2)}) copy-start(f32[128]{0:T(128)} %param.23) | copy-start | bytes 1540
  298.0 17.0 %copy-start.2 = (s32[128]{0:T(128)S(1)}, s32[128]{0:T(128)}, u32[]{:S(2)}) copy-start(s32[128]{0:T(128)} %param.22) | copy-start | bytes 1540
  312.6 3.8 %collective-permute-start.15 = (bf16[128,6400]{1,0:T(8,128)(2,1)}, bf16[128,6400]{1,0:T(8,128)(2,1)}, u32[]{:S(2)}, u32[]{:S(2)}) collective-permute-start(bf16[128,6400]{1,0:T(8,128)(2,1)} %get-tuple-element.14), channel_id=1, source_target_pairs={{0,16},{16,0},{1,17},{17,1},{2,18},{18,2},{3,19},{19,3},{4,20},{20... | collective-permute-start | bytes 4915208 | tf_op jit(solution)/shard_map/ppermute | solution.py:12
Sparse Core Ops, SparseCore 0:
  188.7 107.5 all-reduce.1
